TPU v7x, 32 devices: a whole 2x2x4 slice. The times are simulated.
32 devices in a mesh: row: 4 (over z), col: 8 (over y, x, core).
Axes of the slice: x: 2, y: 2, z: 4, core: 2. Of those that a mesh axis runs over, the one named last changes fastest.
Arguments:
- matrix_tiles: float32 [4, 8, 16, 512, 512], P('row', 'col'), may hold values from -0.25 to 0.25
- tile_rows: int32 [4, 8, 16], P('row', 'col'), may hold values from 0 to 63, as said below
- tile_columns: int32 [4, 8, 16], P('row', 'col'), may hold values from 0 to 31, as said below
- tile_counts: int32 [4, 8], P('row', 'col'), may hold values from 8 to 16, as said below
- primal_iter: float32 [2, 131072], P(None, ('col', 'row')), may hold values from -6 to 6
- dual_iter: float32 [2, 131072], P(None, ('row', 'col')), may hold values from -6 to 6
- requirement: float32 [131072], P('row'), may hold values from -68 to 68
- constraint_kind: int32 [131072], P('row'), may hold values from 0 to 1
- objective: float32 [131072], P('col'), may hold values from -68 to 68
- lower_bound: float32 [131072], P('col'), may hold values from -1.5 to 1.5
- upper_bound: float32 [131072], P('col'), may hold values from -1.5 to 1.5
- variable_kind: int32 [131072], P('col'), may hold values from 0 to 3
Outputs:
- primal_residual: float32 [2, 131072], P(None, ('row', 'col'))
- dual_residual: float32 [2, 131072], P(None, ('col', 'row'))
- metrics: float32 [2, 3], replicated
Inputs may be any that keep to these rules, and one draw needn't show every extreme that they name: `tile_counts`: slots below the count of a list hold live tiles, the others are padding; some list has all 16 slots live. `tile_rows`: in each constraint group, the first (8) slots of its lists name every block row of the group exactly once; later slots name any block row, and repeated tiles add. `tile_columns`: in each variable group, the first (8) slots of its lists name every block column of the group exactly once; later slots name any block column, and repeated tiles add. `constraint_kind`: 0 marks an equality, 1 a constraint of the form at least. `variable_kind`: 0 free, 1 lower bound only, 2 upper bound only, 3 both bounds.
All inputs are finite; a program needn't handle non-finite values.
Results may differ from a plain program's by a relative error of at most 0.0003.
Values sent between devices are 32-bit elements; how exact they have to be, the bound alone decides.
No kernel may reach another device: no remote copies, remote signals or barrier semaphores. Data moves between devices by JAX's collectives and lax.ppermute only.
A program may use at most 64 MiB of HBM per device.

v0:
```python
import jax
import jax.numpy as jnp
from jax import lax
from jax.sharding import PartitionSpec as P

HIGHEST_PRECISION = lax.Precision.HIGHEST


def primal_side(product, require_part, kind_part, dual_part):
    difference = require_part[None, :] - product
    residual = jnp.where(kind_part[None, :] == 1, jnp.maximum(difference, 0.0), difference)
    return (
        residual,
        jnp.sum(residual * residual, axis=1),
        jnp.sum(require_part * require_part),
        jnp.sum(require_part[None, :] * dual_part, axis=1),
    )


def dual_side(transposed, objective, lower_bound, upper_bound, variable_kind, primal_part):
    reduced = objective[None, :] - transposed
    lower_active = (variable_kind == 1) | (variable_kind == 3)
    upper_active = (variable_kind == 2) | (variable_kind == 3)
    multiplier = jnp.where(lower_active[None, :], jnp.maximum(reduced, 0.0), 0.0) + jnp.where(
        upper_active[None, :], jnp.minimum(reduced, 0.0), 0.0
    )
    residual = reduced - multiplier
    bound_sum = jnp.sum(
        lower_bound[None, :] * jnp.maximum(multiplier, 0.0)
        + upper_bound[None, :] * jnp.minimum(multiplier, 0.0),
        axis=1,
    )
    return (
        residual,
        jnp.sum(residual * residual, axis=1),
        jnp.sum(objective * objective),
        jnp.sum(objective[None, :] * primal_part, axis=1),
        bound_sum,
    )


def finish(
    primal_square,
    require_square,
    require_dot,
    dual_square,
    objective_square,
    objective_dot,
    bound_sum,
):
    primal_ratio = jnp.sqrt(primal_square) / (1.0 + jnp.sqrt(require_square))
    dual_ratio = jnp.sqrt(dual_square) / (1.0 + jnp.sqrt(objective_square))
    dual_value = require_dot + bound_sum
    duality_gap = jnp.abs(objective_dot - dual_value) / (
        1.0 + jnp.abs(objective_dot) + jnp.abs(dual_value)
    )
    return jnp.stack([primal_ratio, dual_ratio, duality_gap], axis=1)


def on_device(
    matrix_tiles,
    tile_rows,
    tile_columns,
    tile_counts,
    primal_iter,
    dual_iter,
    requirement,
    constraint_kind,
    objective,
    lower_bound,
    upper_bound,
    variable_kind,
):
    own_tiles = matrix_tiles[0, 0]
    slot_count = own_tiles.shape[0]
    block_size = own_tiles.shape[-1]
    candidates = primal_iter.shape[0]
    active = (lax.iota(jnp.int32, slot_count) < tile_counts[0, 0]).astype(jnp.float32)
    primal_group = lax.all_gather(primal_iter, "row", axis=1, tiled=True)
    dual_group = lax.all_gather(dual_iter, "col", axis=1, tiled=True)
    column_blocks = primal_group.shape[1] // block_size
    row_blocks = dual_group.shape[1] // block_size
    column_pick = (
        tile_columns[0, 0][:, None] == lax.iota(jnp.int32, column_blocks)[None, :]
    ).astype(jnp.float32)
    column_pick = column_pick * active[:, None]
    row_pick = (tile_rows[0, 0][:, None] == lax.iota(jnp.int32, row_blocks)[None, :]).astype(
        jnp.float32
    )
    row_pick = row_pick * active[:, None]
    primal_pick = jnp.einsum(
        "tc,scb->stb",
        column_pick,
        primal_group.reshape(candidates, column_blocks, block_size),
        precision=HIGHEST_PRECISION,
    )
    dual_pick = jnp.einsum(
        "tr,srb->stb",
        row_pick,
        dual_group.reshape(candidates, row_blocks, block_size),
        precision=HIGHEST_PRECISION,
    )
    tile_product = jnp.einsum("tij,stj->tsi", own_tiles, primal_pick, precision=HIGHEST_PRECISION)
    tile_transposed = jnp.einsum("tij,sti->tsj", own_tiles, dual_pick, precision=HIGHEST_PRECISION)
    row_share = dual_iter.shape[1]
    column_share = primal_iter.shape[1]
    row_start = lax.axis_index("col") * row_share
    column_start = lax.axis_index("row") * column_share
    product_part = jnp.einsum(
        "tr,tsi->sri", row_pick, tile_product, precision=HIGHEST_PRECISION
    ).reshape(candidates, row_blocks * block_size)
    transposed_part = jnp.einsum(
        "tc,tsj->scj", column_pick, tile_transposed, precision=HIGHEST_PRECISION
    ).reshape(candidates, column_blocks * block_size)
    product = lax.psum(product_part, "col")
    transposed = lax.psum(transposed_part, "row")
    primal_full, primal_square, require_square, require_dot = primal_side(
        product, requirement, constraint_kind, dual_group
    )
    primal_square, require_square, require_dot = lax.psum(
        (primal_square, require_square, require_dot), "row"
    )
    dual_full, dual_square, objective_square, objective_dot, bound_sum = dual_side(
        transposed, objective, lower_bound, upper_bound, variable_kind, primal_group
    )
    dual_square, objective_square, objective_dot, bound_sum = lax.psum(
        (dual_square, objective_square, objective_dot, bound_sum), "col"
    )
    primal_residual = lax.dynamic_slice_in_dim(primal_full, row_start, row_share, 1)
    dual_residual = lax.dynamic_slice_in_dim(dual_full, column_start, column_share, 1)
    metrics = finish(
        primal_square,
        require_square,
        require_dot,
        dual_square,
        objective_square,
        objective_dot,
        bound_sum,
    )
    return (primal_residual, dual_residual, metrics)


def solution(mesh):
    placed = (
        P("row", "col", None, None, None),
        P("row", "col", None),
        P("row", "col", None),
        P("row", "col"),
        P(None, ("col", "row")),
        P(None, ("row", "col")),
        P("row"),
        P("row"),
        P("col"),
        P("col"),
        P("col"),
        P("col"),
    )
    return jax.shard_map(
        on_device,
        mesh=mesh,
        in_specs=placed,
        out_specs=(P(None, ("row", "col")), P(None, ("col", "row")), P()),
        check_vma=False,
    )
```

profile of v0, /device:TPU:0, one launch (start us, length us, event | category | flops | bytes accessed | tf_op | source)
XLA Modules:
  0.0 147.8 jit_solution(15917342106605868104)
XLA Ops:
  7.2 0.0 copy-start.7
  7.2 0.0 copy-start.6
  7.2 0.0 all-reduce.7.cloned.1.call-start
  7.9 11.0 %all_gather.7 = f32[2,32768]{1,0:T(2,128)S(1)} all-gather(f32[2,4096]{1,0:T(2,128)} %param.17), channel_id=1, replica_groups=mesh['row'=4,'col'=8] {'col'}, dimensions={1}, use_global_device_ids=true | all-gather | bytes 294912 | tf_op jit(solution)/shard_map/all_gather | solution.py:80
  18.9 0.9 fusion.4
  19.8 0.0 copy-start.8
  19.8 0.0 copy-start.3
  19.9 0.0 copy-start.1
  19.9 0.0 copy-start.2
  19.9 0.0 copy-start
  19.9 0.0 copy-start.4
  19.9 0.0 copy-start.5
  19.9 11.6 %fusion = f32[16,2,512]{2,1,0:T(2,128)S(1)} fusion(f32[1,1,16,512,512]{4,3,2,1,0:T(8,128)} %param.12, f32[16,2,512]{2,0,1:T(8,128)S(1)} %fusion.4), kind=kOutput, calls=%fused_computation | convolution fusion | flops 100663296 | bytes 16908288 | tf_op jit(solution)/shard_map/tij,sti->tsj/dot_general | solution.py:104
  31.6 0.0 copy-done.7
  31.6 0.4 convolution_bitcast_fusion.1
  31.9 0.7 copy.23
  32.7 0.0 all-reduce.7.cloned.1.call-update
  32.7 0.0 all-reduce.5.cloned.1.call-start
  32.8 0.0 copy-done.6
  32.8 13.9 %all_gather.6 = f32[2,16384]{1,0:T(2,128)S(1)} all-gather(f32[2,4096]{1,0:T(2,128)S(1)} %copy-done.6), channel_id=1, replica_groups=mesh['row'=4,'col'=8] {'row'}, dimensions={1}, use_global_device_ids=true | all-gather | bytes 163840 | tf_op jit(solution)/shard_map/all_gather | solution.py:79
  46.7 0.3 fusion.7
  46.9 17.2 %fusion.2 = f32[16,2,512]{2,1,0:T(2,128)S(1)} fusion(f32[1,1,16,512,512]{4,3,2,1,0:T(8,128)} %param.12, f32[16,2,512]{2,0,1:T(8,128)S(1)} %fusion.7), kind=kOutput, calls=%fused_computation.2 | convolution fusion | flops 100663296 | bytes 16908288 | tf_op jit(solution)/shard_map/tij,stj->tsi/dot_general | solution.py:103
  64.1 0.0 copy-done.8
  64.1 0.5 convolution_bitcast_fusion
  64.6 0.9 copy.21
  65.5 0.0 all-reduce.5.cloned.1.call-update
  65.6 0.0 copy-done.3
  65.6 0.0 copy-done.1
  65.6 0.6 multiply_reduce_fusion.5
  66.2 0.0 copy-done.2
  66.3 0.0 copy-done
  66.3 0.6 multiply_reduce_fusion.4
  66.9 1.0 all-reduce.7.cloned.1.call-done
  67.9 0.0 copy-done.4
  67.9 0.0 copy-done.5
  67.9 1.5 add_reduce_fusion
  69.4 12.5 %all-reduce = (f32[2]{0:T(128)S(1)}, f32[2]{0:T(128)S(1)}, f32[2]{0:T(128)S(1)}, f32[]{:T(128)}) all-reduce(f32[2]{0:T(128)S(1)} %get-tuple-element.7, f32[2]{0:T(128)S(1)} %get-tuple-element.6, f32[2]{0:T(128)S(1)} %get-tuple-element.19, f32[]{:T(128)} %multiply_reduce_fusion.5), channel_id=1, replica_groups=mesh['row'=4,'col'=8] {'col'}, use_global_device_ids=true, to_apply=%region_11.12 | all-reduce | flops 7 | bytes 56 | tf_op jit(solution)/shard_map/psum | solution.py:126
  82.6 41.9 %all-reduce.5.cloned.1.call-done = f32[2,32768]{1,0:T(2,128)} async-done(((f32[2,32768]{1,0:T(2,128)}), f32[2,32768]{1,0:T(2,128)}) %all-reduce.5.cloned.1.call-update) | async-done | bytes 262160 | tf_op jit(solution)/shard_map/psum | solution.py:115
  124.5 1.5 %multiply_reduce_fusion.1 = (f32[2]{0:T(128)S(1)}, f32[2,32768]{1,0:T(2,128)S(1)}, f32[2]{0:T(128)S(1)}) fusion(f32[2,32768]{1,0:T(2,128)} %all-reduce.5.cloned.1.call-done, f32[32768]{0:T(1024)S(1)} %copy-done, pred[32768]{0:T(1024)(128)(4,1)S(1)} %broadcast_compare_fusion, f32[2,32768]{1,0:T(2,128)S(1)} %all_gather.7), kind=kLoop, calls=%fused_computation.11 | loop fusion | flops 458748 | bytes 950288 | tf_op jit(solution)/shard_map/reduce_sum | solution.py:14
  126.0 12.3 %all-reduce.1 = (f32[2]{0:T(128)S(1)}, f32[2]{0:T(128)S(1)}, f32[]{:T(128)}) all-reduce(f32[2]{0:T(128)S(1)} %get-tuple-element.21, f32[2]{0:T(128)S(1)} %get-tuple-element.15, f32[]{:T(128)} %multiply_reduce_fusion.4), channel_id=1, replica_groups=mesh['row'=4,'col'=8] {'row'}, use_global_device_ids=true, to_apply=%region_13.14 | all-reduce | flops 5 | bytes 40 | tf_op jit(solution)/shard_map/psum | solution.py:120
  139.1 0.6 copy.15
  139.8 0.6 constant_dynamic-slice_fusion
  140.4 0.6 constant_dynamic-slice_fusion.1
  (7 shorter events, 0.1 us)
Async XLA Ops:
  7.2 24.4 %copy-start.7 = (s32[1,1,16]{2,1,0:T(1,128)S(1)}, s32[1,1,16]{2,1,0:T(1,128)}, u32[]{:S(2)}) copy-start(s32[1,1,16]{2,1,0:T(1,128)} %param.14) | copy-start | bytes 196
  7.2 25.6 %copy-start.6 = (f32[2,4096]{1,0:T(2,128)S(1)}, f32[2,4096]{1,0:T(2,128)}, u32[]{:S(2)}) copy-start(f32[2,4096]{1,0:T(2,128)} %param.16) | copy-start | bytes 98308
  7.2 60.7 %all-reduce.7.cloned.1.call-start = ((), (), s32[]{:S(2)}) async-start(), calls=%async_computation.1 | async-start | bytes 262144 | tf_op jit(solution)/shard_map/psum | solution.py:116
  19.8 44.3 %copy-start.8 = (s32[1,1,16]{2,1,0:T(1,128)S(1)}, s32[1,1,16]{2,1,0:T(1,128)}, u32[]{:S(2)}) copy-start(s32[1,1,16]{2,1,0:T(1,128)} %param.13) | copy-start | bytes 196
  19.8 45.7 %copy-start.3 = (s32[16384]{0:T(1024)S(1)}, s32[16384]{0:T(1024)}, u32[]{:S(2)}) copy-start(s32[16384]{0:T(1024)} %param.23) | copy-start | bytes 196612
  19.9 45.8 %copy-start.1 = (f32[16384]{0:T(1024)S(1)}, f32[16384]{0:T(1024)}, u32[]{:S(2)}) copy-start(f32[16384]{0:T(1024)} %param.20) | copy-start | bytes 196612
  19.9 46.4 %copy-start.2 = (s32[32768]{0:T(1024)S(1)}, s32[32768]{0:T(1024)}, u32[]{:S(2)}) copy-start(s32[32768]{0:T(1024)} %param.19) | copy-start | bytes 393220
  19.9 46.4 %copy-start = (f32[32768]{0:T(1024)S(1)}, f32[32768]{0:T(1024)}, u32[]{:S(2)}) copy-start(f32[32768]{0:T(1024)} %param.18) | copy-start | bytes 393220
  19.9 48.0 %copy-start.4 = (f32[16384]{0:T(1024)S(1)}, f32[16384]{0:T(1024)}, u32[]{:S(2)}) copy-start(f32[16384]{0:T(1024)} %param.22) | copy-start | bytes 196612
  19.9 48.0 %copy-start.5 = (f32[16384]{0:T(1024)S(1)}, f32[16384]{0:T(1024)}, u32[]{:S(2)}) copy-start(f32[16384]{0:T(1024)} %param.21) | copy-start | bytes 196612
  32.7 91.8 %all-reduce.5.cloned.1.call-start = ((), (), s32[]{:S(2)}) async-start(), calls=%async_computation | async-start | bytes 524288 | tf_op jit(solution)/shard_map/psum | solution.py:115
Sparse Core Ops, SparseCore 0:
  32.8 35.0 all-reduce.6
  71.0 53.5 all-reduce.4
where the time goes:
time: 148 us
  blocking collectives  49.8 us (34%)
  waiting for transfers between devices  43 us (29%)
  matrix products  30.9 us (21%)
  between operations  16.3 us (11%)
  other arithmetic  4.29 us (3%)
  local copies, waits for them, and re-layouts  3.58 us (2%)
    psum x1, waiting for transfers between devices, on_device(): product = lax.psum(product_part, 'col')  41.9 us
    dot_general x1, matrix products, on_device(): jnp.einsum('tij,stj->tsi', own_tiles, primal_pick, precision=HIGHEST_PREC...  17.2 us
    all_gather x1, blocking collectives, on_device(): primal_group = lax.all_gather(primal_iter, 'row', axis=1, tiled=True)  13.9 us
    psum x1, blocking collectives, on_device(): lax.psum((dual_square, objective_square, objective_dot, bound_sum), 'col')  12.5 us
    psum x1, blocking collectives, on_device(): lax.psum((primal_square, require_square, require_dot), 'row')  12.3 us
    dot_general x1, matrix products, on_device(): jnp.einsum('tij,sti->tsj', own_tiles, dual_pick, precision=HIGHEST_PRECIS...  11.6 us
    all_gather x1, blocking collectives, on_device(): dual_group = lax.all_gather(dual_iter, 'col', axis=1, tiled=True)  11 us
  transfers between devices with their start and end apart: 2, of which 2 were waited for; matrix products, arithmetic and copies ran while one was open for 15% of the time, Pallas kernels for 0%

commit v1 on v0

--- a/solution.py
+++ b/solution.py
@@ -112,7 +112,7 @@
     transposed_part = jnp.einsum(
         "tc,tsj->scj", column_pick, tile_transposed, precision=HIGHEST_PRECISION
     ).reshape(candidates, column_blocks * block_size)
-    product = lax.psum(product_part, "col")
+    product = jnp.sum(lax.all_gather(product_part, "col"), axis=0)
     transposed = lax.psum(transposed_part, "row")
     primal_full, primal_square, require_square, require_dot = primal_side(
         product, requirement, constraint_kind, dual_group

time: 148 us -> 120 us (0.81)
  waiting for transfers between devices: 43 us -> 11.4 us
  other arithmetic: 4.29 us -> 5.87 us
    psum x1 -> x0, waiting for transfers between devices: 41.9 us -> none  [on_device(): product = lax.psum(product_part, 'col')]
    all_gather x0 -> x1, waiting for transfers between devices: none -> 10.6 us  [on_device(): product = jnp.sum(lax.all_gather(product_part, 'col'), axis=0)]
    reduce_sum x0 -> x1, other arithmetic: none -> 2.36 us  [on_device(): product = jnp.sum(lax.all_gather(product_part, 'col'), axis=0)]
  transfers between devices with their start and end apart: 2 -> 2, of which waited for: 2 -> 2; matrix products, arithmetic and copies ran while one was open for 15% -> 19% of each run, Pallas kernels for 0% -> 0%
where the time goes in v1:
time: 120 us; the launch traced here: 119 us
  blocking collectives  49.7 us (41%)
  matrix products  30.9 us (26%)
  between operations  17.7 us (15%)
  waiting for transfers between devices  11.4 us (10%)
  other arithmetic  5.87 us (5%)
  local copies, waits for them, and re-layouts  3.64 us (3%)
    dot_general x1, matrix products, on_device(): jnp.einsum('tij,stj->tsi', own_tiles, primal_pick, precision=HIGHEST_PREC...  17.2 us
    all_gather x1, blocking collectives, on_device(): primal_group = lax.all_gather(primal_iter, 'row', axis=1, tiled=True)  13.9 us
    psum x1, blocking collectives, on_device(): lax.psum((dual_square, objective_square, objective_dot, bound_sum), 'col')  12.5 us
    psum x1, blocking collectives, on_device(): lax.psum((primal_square, require_square, require_dot), 'row')  12.3 us
    dot_general x1, matrix products, on_device(): jnp.einsum('tij,sti->tsj', own_tiles, dual_pick, precision=HIGHEST_PRECIS...  11.6 us
    all_gather x1, blocking collectives, on_device(): dual_group = lax.all_gather(dual_iter, 'col', axis=1, tiled=True)  11 us
    all_gather x1, waiting for transfers between devices, on_device(): product = jnp.sum(lax.all_gather(product_part, 'col'), axis=0)  10.6 us
  transfers between devices with their start and end apart: 2, of which 2 were waited for; matrix products, arithmetic and copies ran while one was open for 19% of the time, Pallas kernels for 0%

profile of v1, /device:TPU:0, one launch (start us, length us, event | category | flops | bytes accessed | tf_op | source)
XLA Modules:
  0.0 119.4 jit_solution(16442229243700933055)
XLA Ops:
  8.0 0.0 copy-start.7
  8.0 0.0 copy-start.6
  8.0 0.0 all-reduce.4.cloned.1.call-start
  8.7 11.0 %all_gather.11 = f32[2,32768]{1,0:T(2,128)S(1)} all-gather(f32[2,4096]{1,0:T(2,128)} %param.17), channel_id=1, replica_groups=mesh['row'=4,'col'=8] {'col'}, dimensions={1}, use_global_device_ids=true | all-gather | bytes 294912 | tf_op jit(solution)/shard_map/all_gather | solution.py:80
  19.7 0.9 fusion.4
  20.7 0.0 copy-start.8
  20.7 0.0 copy-start.1
  20.7 0.0 copy-start
  20.7 0.0 copy-start.3
  20.7 0.0 copy-start.2
  20.7 0.0 copy-start.4
  20.7 0.0 copy-start.5
  20.8 11.6 %fusion = f32[16,2,512]{2,1,0:T(2,128)S(1)} fusion(f32[1,1,16,512,512]{4,3,2,1,0:T(8,128)} %param.12, f32[16,2,512]{2,0,1:T(8,128)S(1)} %fusion.4), kind=kOutput, calls=%fused_computation | convolution fusion | flops 100663296 | bytes 16908288 | tf_op jit(solution)/shard_map/tij,sti->tsj/dot_general | solution.py:104
  32.4 0.0 copy-done.7
  32.4 0.4 convolution_bitcast_fusion.1
  32.8 0.8 copy.23
  33.5 0.0 all-reduce.4.cloned.1.call-update
  33.6 0.0 all-gather.2.cloned.1.call-start
  33.6 0.0 copy-done.6
  33.6 13.9 %all_gather.9 = f32[2,16384]{1,0:T(2,128)S(1)} all-gather(f32[2,4096]{1,0:T(2,128)S(1)} %copy-done.6), channel_id=1, replica_groups=mesh['row'=4,'col'=8] {'row'}, dimensions={1}, use_global_device_ids=true | all-gather | bytes 163840 | tf_op jit(solution)/shard_map/all_gather | solution.py:79
  47.5 0.3 fusion.7
  47.8 17.2 %fusion.2 = f32[16,2,512]{2,1,0:T(2,128)S(1)} fusion(f32[1,1,16,512,512]{4,3,2,1,0:T(8,128)} %param.12, f32[16,2,512]{2,0,1:T(8,128)S(1)} %fusion.7), kind=kOutput, calls=%fused_computation.2 | convolution fusion | flops 100663296 | bytes 16908288 | tf_op jit(solution)/shard_map/tij,stj->tsi/dot_general | solution.py:103
  65.0 0.0 copy-done.8
  65.0 0.5 convolution_bitcast_fusion
  65.5 0.9 all_gather_reshape.3
  66.4 0.0 all-gather.2.cloned.1.call-update
  66.5 0.0 copy-done.1
  66.5 0.6 multiply_reduce_fusion.5
  67.1 0.0 copy-done
  67.1 0.6 multiply_reduce_fusion.4
  67.7 0.0 copy-done.3
  67.8 0.0 copy-done.2
  67.8 0.8 all-reduce.4.cloned.1.call-done
  68.7 0.0 copy-done.4
  68.7 0.0 copy-done.5
  68.7 1.5 %add_reduce_fusion = (f32[2]{0:T(128)S(1)}, f32[2]{0:T(128)S(1)}, f32[2]{0:T(128)S(1)}, f32[2,16384]{1,0:T(2,128)S(1)}) fusion(f32[16384]{0:T(1024)S(1)} %copy-done.4, f32[16384]{0:T(1024)S(1)} %copy-done.5, pred[16384]{0:T(1024)(128)(4,1)S(1)} %get-tuple-element.26, f32[2,16384]{1,0:T(2,128)} %all-reduce.4.cloned.1.call-done, f32[16384]{0:T(1024)S(1)} %copy-done.1, ...), kind=kLoop, calls=%fused_computation.15 | loop fusion | flops 557050 | bytes 622616 | tf_op jit(solution)/shard_map/reduce_sum | solution.py:28
  70.1 12.5 %all-reduce = (f32[2]{0:T(128)S(1)}, f32[2]{0:T(128)S(1)}, f32[2]{0:T(128)S(1)}, f32[]{:T(128)}) all-reduce(f32[2]{0:T(128)S(1)} %get-tuple-element.10, f32[2]{0:T(128)S(1)} %get-tuple-element.9, f32[2]{0:T(128)S(1)} %get-tuple-element.22, f32[]{:T(128)} %multiply_reduce_fusion.5), channel_id=1, replica_groups=mesh['row'=4,'col'=8] {'col'}, use_global_device_ids=true, to_apply=%region_11.12 | all-reduce | flops 7 | bytes 56 | tf_op jit(solution)/shard_map/psum | solution.py:126
  83.3 0.6 constant_dynamic-slice_fusion
  84.0 10.6 %all-gather.2.cloned.1.call-done = f32[8,2,32768]{2,1,0:T(2,128)} async-done(((f32[1,2,32768]{2,1,0:T(2,128)}), f32[8,2,32768]{2,1,0:T(2,128)}) %all-gather.2.cloned.1.call-update) | async-done | bytes 2097168 | tf_op jit(solution)/shard_map/all_gather | solution.py:115
  94.5 2.4 %reduce_sum.72 = f32[2,32768]{1,0:T(2,128)S(1)} reduce(f32[8,2,32768]{2,1,0:T(2,128)} %all-gather.2.cloned.1.call-done, f32[]{:T(128)} %constant.12.clone.1), dimensions={0}, to_apply=%region_0.0 | reduce | flops 458752 | bytes 2359300 | tf_op jit(solution)/shard_map/reduce_sum | solution.py:115
  96.9 0.7 multiply_reduce_fusion.1
  97.6 12.3 %all-reduce.1 = (f32[2]{0:T(128)S(1)}, f32[2]{0:T(128)S(1)}, f32[]{:T(128)}) all-reduce(f32[2]{0:T(128)S(1)} %get-tuple-element.24, f32[2]{0:T(128)S(1)} %get-tuple-element.18, f32[]{:T(128)} %multiply_reduce_fusion.4), channel_id=1, replica_groups=mesh['row'=4,'col'=8] {'row'}, use_global_device_ids=true, to_apply=%region_13.14 | all-reduce | flops 5 | bytes 40 | tf_op jit(solution)/shard_map/psum | solution.py:120
  110.7 0.6 copy.16
  111.3 0.6 constant_dynamic-slice_fusion.1
  (7 shorter events, 0.1 us)
Async XLA Ops:
  8.0 24.4 %copy-start.7 = (s32[1,1,16]{2,1,0:T(1,128)S(1)}, s32[1,1,16]{2,1,0:T(1,128)}, u32[]{:S(2)}) copy-start(s32[1,1,16]{2,1,0:T(1,128)} %param.14) | copy-start | bytes 196
  8.0 25.6 %copy-start.6 = (f32[2,4096]{1,0:T(2,128)S(1)}, f32[2,4096]{1,0:T(2,128)}, u32[]{:S(2)}) copy-start(f32[2,4096]{1,0:T(2,128)} %param.16) | copy-start | bytes 98308
  8.0 60.6 %all-reduce.4.cloned.1.call-start = ((), (), s32[]{:S(2)}) async-start(), calls=%async_computation.1 | async-start | bytes 262144 | tf_op jit(solution)/shard_map/psum | solution.py:116
  20.7 44.3 %copy-start.8 = (s32[1,1,16]{2,1,0:T(1,128)S(1)}, s32[1,1,16]{2,1,0:T(1,128)}, u32[]{:S(2)}) copy-start(s32[1,1,16]{2,1,0:T(1,128)} %param.13) | copy-start | bytes 196
  20.7 45.8 %copy-start.1 = (f32[16384]{0:T(1024)S(1)}, f32[16384]{0:T(1024)}, u32[]{:S(2)}) copy-start(f32[16384]{0:T(1024)} %param.20) | copy-start | bytes 196612
  20.7 46.4 %copy-start = (f32[32768]{0:T(1024)S(1)}, f32[32768]{0:T(1024)}, u32[]{:S(2)}) copy-start(f32[32768]{0:T(1024)} %param.18) | copy-start | bytes 393220
  20.7 47.0 %copy-start.3 = (s32[16384]{0:T(1024)S(1)}, s32[16384]{0:T(1024)}, u32[]{:S(2)}) copy-start(s32[16384]{0:T(1024)} %param.23) | copy-start | bytes 196612
  20.7 47.1 %copy-start.2 = (s32[32768]{0:T(1024)S(1)}, s32[32768]{0:T(1024)}, u32[]{:S(2)}) copy-start(s32[32768]{0:T(1024)} %param.19) | copy-start | bytes 393220
  20.7 47.9 %copy-start.4 = (f32[16384]{0:T(1024)S(1)}, f32[16384]{0:T(1024)}, u32[]{:S(2)}) copy-start(f32[16384]{0:T(1024)} %param.22) | copy-start | bytes 196612
  20.7 47.9 %copy-start.5 = (f32[16384]{0:T(1024)S(1)}, f32[16384]{0:T(1024)}, u32[]{:S(2)}) copy-start(f32[16384]{0:T(1024)} %param.21) | copy-start | bytes 196612
  33.6 61.0 %all-gather.2.cloned.1.call-start = ((), (), s32[]{:S(2)}) async-start(), calls=%async_computation | async-start | bytes 2359296 | tf_op jit(solution)/shard_map/all_gather | solution.py:115
Sparse Core Ops, SparseCore 0:
  33.7 34.9 all-reduce.3
Sparse Core Ops, SparseCore 1:
  66.6 27.9 all-gather.1
